TPU v7x, 256 devices: a whole 4x4x8 slice. The times are simulated.
256 devices in a mesh: fsdp: 64 (over z_lo, x, y, core), tensor: 4 (over z_hi).
Axes of the slice: x: 4, y: 4, z: 8 (z_hi: 4, z_lo: 2; z = z_hi * 2 + z_lo), core: 2. Of those that a mesh axis runs over, the one named last changes fastest.
Arguments:
- normed: bfloat16 [65536, 8192], P('fsdp', 'tensor')
- tile_values: bfloat16 [4, 128, 128, 128], P('tensor', 'fsdp'), may hold values from -0.09375 to 0.09375
- tile_rows: int32 [4, 128], P('tensor', 'fsdp'), may hold values from -1 to 15, as said below
- tile_columns: int32 [4, 128], P('tensor', 'fsdp'), may hold values from -1 to 7, as said below
- cotangent: bfloat16 [65536, 1024], P('fsdp', 'tensor')
Outputs:
- values: bfloat16 [65536, 1024], P('fsdp', 'tensor')
- grad_input: bfloat16 [65536, 8192], P('fsdp', 'tensor')
- tile_update: bfloat16 [4, 128, 128, 128], P('tensor', 'fsdp')
Inputs may be any that keep to these rules, and one draw needn't show every extreme that they name: tile_rows[q, s] is -1 exactly where tile_columns[q, s] is -1 (an empty slot). In every part q exactly 64 slots are filled, no (row block, column block) pair appears twice, and each column block holds exactly 8 of the 16 row blocks. The slots s with equal s // 2 belong to one owner; in every part some owner has all 2 of its slots filled. `tile_columns`: column block of the tile in each slot; -1 marks an empty slot, as in tile_rows.
All inputs are finite; a program needn't handle non-finite values.
Results may differ from a plain program's by a relative error of at most 0.001.
Values may be sent and summed in bfloat16 or wider, within the bound.
A program may use at most 128 MiB of HBM per device.

v0:
```python
import jax
import jax.numpy as jnp
from jax import lax
from jax.sharding import PartitionSpec as P


def normalize(summed):
    inverse_rms = lax.rsqrt(jnp.mean(summed * summed, axis=(1, 2), keepdims=True) + 1e-06)
    return (summed * inverse_rms).astype(jnp.bfloat16)


def local(normed, tile_values, tile_rows, tile_columns, cotangent):
    feature_width = normed.shape[1]
    tile_size = tile_values.shape[-1]
    row_blocks = feature_width // tile_size
    gathered_values, gathered_rows, gathered_columns = (
        lax.all_gather(tile_values, "fsdp", axis=1, tiled=True),
        lax.all_gather(tile_rows, "fsdp", axis=1, tiled=True),
        lax.all_gather(tile_columns, "fsdp", axis=1, tiled=True),
    )
    gathered_values = gathered_values[0]
    gathered_rows = gathered_rows[0]
    gathered_columns = gathered_columns[0]
    full_cotangent = lax.all_gather(cotangent, "tensor", axis=1, tiled=True)
    column_blocks = full_cotangent.shape[1] // tile_size
    pair_total = row_blocks * column_blocks
    occupied = gathered_columns >= 0
    pair_index = jnp.where(occupied, gathered_rows * column_blocks + gathered_columns, 0)
    pair_hot = (
        (pair_index[:, None] == jnp.arange(pair_total, dtype=jnp.int32)[None, :])
        & occupied[:, None]
    ).astype(jnp.bfloat16)
    blocks = jnp.einsum(
        "sp,sij->pij", pair_hot, gathered_values, preferred_element_type=jnp.float32
    ).astype(jnp.bfloat16)
    weight = (
        blocks.reshape(row_blocks, column_blocks, tile_size, tile_size)
        .transpose(0, 2, 1, 3)
        .reshape(feature_width, column_blocks * tile_size)
    )
    partial_value = jnp.dot(normed, weight, preferred_element_type=jnp.float32)
    values = lax.psum_scatter(partial_value, "tensor", scatter_dimension=1, tiled=True).astype(
        jnp.bfloat16
    )
    grad_input = jnp.einsum(
        "tk,dk->td", full_cotangent, weight, preferred_element_type=jnp.float32
    ).astype(jnp.bfloat16)
    gradient = jnp.einsum("td,tk->dk", normed, full_cotangent, preferred_element_type=jnp.float32)
    grad_pairs = (
        gradient.reshape(row_blocks, tile_size, column_blocks, tile_size)
        .transpose(0, 2, 1, 3)
        .reshape(pair_total, tile_size, tile_size)
    )
    summed = lax.psum_scatter(
        jnp.where(occupied[:, None, None], jnp.take(grad_pairs, pair_index, axis=0), 0.0),
        "fsdp",
        scatter_dimension=0,
        tiled=True,
    )
    tile_update = normalize(summed)
    return (values, grad_input, tile_update[None])


def solution(mesh):
    in_specs = (
        P("fsdp", "tensor"),
        P("tensor", "fsdp", None, None),
        P("tensor", "fsdp"),
        P("tensor", "fsdp"),
        P("fsdp", "tensor"),
    )
    out_specs = (P("fsdp", "tensor"), P("fsdp", "tensor"), P("tensor", "fsdp", None, None))
    return jax.shard_map(local, mesh=mesh, in_specs=in_specs, out_specs=out_specs, check_vma=False)
```

profile of v0, /device:TPU:1, one launch (start us, length us, event | category | flops | bytes accessed | tf_op | source)
XLA Modules:
  0.0 569.2 jit_solution(7977456450742726199)
XLA Ops:
  7.2 0.0 all-gather.3.cloned.1.call-start
  7.2 0.7 all-gather.3.cloned.1.call-update
  7.9 0.0 all-gather.5.cloned.1.call-start
  7.9 0.7 all-gather.5.cloned.1.call-update
  8.6 0.0 reduce-scatter.3.cloned.1.call-start
  8.7 1.3 dynamic-slice
  10.6 0.8 bitcast_dynamic-update-slice_fusion
  11.4 0.7 bitcast_dynamic-update-slice_fusion.1
  12.1 17.4 %all-reduce.2 = (s32[128]{0:T(128)S(1)}, s32[128]{0:T(128)S(1)}) all-reduce(s32[128]{0:T(128)S(1)} %bitcast_dynamic-update-slice_fusion.1, s32[128]{0:T(128)S(1)} %bitcast_dynamic-update-slice_fusion), channel_id=1, replica_groups=mesh['fsdp'=64,'tensor'=4] {'fsdp'}, use_global_device_ids=true, to_apply=%add | all-reduce | flops 256 | bytes 2048
  29.5 93.0 %all-gather.3.cloned.1.call-done = bf16[1,128,128,128]{3,2,0,1:T(8,128)(2,1)} async-done(((bf16[1,2,128,128]{3,2,0,1:T(8,128)(2,1)}), bf16[1,128,128,128]{3,2,0,1:T(8,128)(2,1)}) %all-gather.3.cloned.1.call-update) | async-done | bytes 4194320 | tf_op jit(solution)/shard_map/all_gather | solution.py:17
  122.5 5.6 convert_bitcast_fusion.1
  128.1 0.0 copy-start.1
  128.2 1.1 copy.18
  129.2 0.0 copy-start
  129.3 2.0 copy-done
  131.3 0.0 copy-done.1
  131.3 6.1 %fusion.13 = f32[1024,1024]{0,1:T(8,128)} fusion(bf16[1024,2048]{1,0:T(8,128)(2,1)S(1)} %copy-done.1, bf16[256,8,8,128]{3,2,1,0:T(8,128)(2,1)S(1)} %bitcast.51), kind=kOutput, calls=%fused_computation.14 | convolution fusion | flops 4294967296 | bytes 12582912 | tf_op jit(solution)/shard_map/dot_general | solution.py:41
  137.4 0.0 reduce-scatter.3.cloned.1.call-update
  137.4 0.2 reduce-scatter.5.cloned.1.call-start
  137.7 40.5 %all-gather.5.cloned.1.call-done = bf16[1024,1024]{1,0:T(8,128)(2,1)} async-done(((bf16[1024,256]{1,0:T(8,128)(2,1)}), bf16[1024,1024]{1,0:T(8,128)(2,1)}) %all-gather.5.cloned.1.call-update) | async-done | bytes 2097168 | tf_op jit(solution)/shard_map/all_gather | solution.py:24
  178.2 7.1 %convolution_bitcast_fusion = f32[256,8,8,128]{3,1,2,0:T(8,128)S(1)} fusion(bf16[1024,2048]{1,0:T(8,128)(2,1)} %param.5, bf16[1024,1024]{1,0:T(8,128)(2,1)} %all-gather.5.cloned.1.call-done), kind=kOutput, calls=%fused_computation.13 | convolution fusion | flops 4294967296 | bytes 14680064 | tf_op jit(solution)/shard_map/td,tk->dk/dot_general | solution.py:48
  185.3 2.1 copy.23
  187.4 5.0 copy.19
  192.5 7.7 %gather_fusion = f32[128,128,128]{2,1,0:T(8,128)} fusion(f32[128,128,128]{2,1,0:T(8,128)} %bitcast.49, s32[1024]{0:T(1024)S(1)} %pad_clamp_fusion), kind=kCustom, calls=%fused_computation | custom fusion | bytes 16777728 | tf_op jit(solution)/shard_map/jit(_take)/gather | solution.py:55
  200.1 6.5 %select_select_fusion = f32[128,128,128]{2,1,0:T(8,128)} fusion(f32[128,128,128]{2,1,0:T(8,128)} %gather_fusion, pred[128]{0:T(512)(128)(4,1)S(1)} %get-tuple-element.14, pred[128]{0:T(512)(128)(4,1)S(1)} %get-tuple-element.16), kind=kLoop, calls=%fused_computation.1 | loop fusion | flops 4194304 | bytes 16777472 | tf_op jit(solution)/shard_map/jit(_where)/select_n | solution.py:55
  206.6 0.0 copy-start.2
  206.6 0.0 reduce-scatter.5.cloned.1.call-update
  206.7 1.6 copy-done.2
  208.2 8.5 %convert_bitcast_fusion = bf16[1024,2048]{0,1:T(8,128)(2,1)} fusion(bf16[1024,1024]{1,0:T(8,128)(2,1)S(1)} %copy-done.2, bf16[256,8,8,128]{3,2,1,0:T(8,128)(2,1)} %bitcast.52), kind=kOutput, calls=%fused_computation.9 | convolution fusion | flops 4297064448 | bytes 10485760 | tf_op jit(solution)/shard_map/tk,dk->td/dot_general | solution.py:45
  216.7 6.4 %copy.21 = bf16[1024,2048]{1,0:T(8,128)(2,1)} copy(bf16[1024,2048]{0,1:T(8,128)(2,1)} %convert_bitcast_fusion) | data formatting | bytes 8388608
  223.1 40.5 %reduce-scatter.3.cloned.1.call-done = f32[1024,256]{0,1:T(8,128)} async-done(((f32[1024,1024]{0,1:T(8,128)}), f32[1024,256]{0,1:T(8,128)}) %reduce-scatter.3.cloned.1.call-update) | async-done | bytes 1048592 | tf_op jit(solution)/shard_map/reduce_scatter | solution.py:42
  263.6 1.3 convert_element_type.17
  264.9 1.0 copy.20
  265.9 294.1 %reduce-scatter.5.cloned.1.call-done = f32[2,128,128]{2,1,0:T(8,128)} async-done(((f32[128,128,128]{2,1,0:T(8,128)}), f32[2,128,128]{2,1,0:T(8,128)}) %reduce-scatter.5.cloned.1.call-update) | async-done | bytes 131088 | tf_op jit(solution)/shard_map/reduce_scatter | solution.py:54
  560.0 1.0 multiply_reduce_fusion
  561.1 1.6 fusion.16
  (6 shorter events, 0.0 us)
Async XLA Ops:
  7.2 115.4 %all-gather.3.cloned.1.call-start = ((), (), s32[]{:S(2)}) async-start(), calls=%async_computation.2 | async-start | bytes 4259840 | tf_op jit(solution)/shard_map/all_gather | solution.py:17
  7.9 170.3 %all-gather.5.cloned.1.call-start = ((), (), s32[]{:S(2)}) async-start(), calls=%async_computation.4 | async-start | bytes 2621440 | tf_op jit(solution)/shard_map/all_gather | solution.py:24
  8.6 255.0 %reduce-scatter.3.cloned.1.call-start = ((), (), s32[]{:S(2)}) async-start(), calls=%async_computation.3 | async-start | bytes 5242880 | tf_op jit(solution)/shard_map/reduce_scatter | solution.py:42
  128.1 3.1 copy-start.1
  129.2 2.0 copy-start
  137.4 422.6 %reduce-scatter.5.cloned.1.call-start = ((), (), s32[]{:S(2)}) async-start(), calls=%async_computation.5 | async-start | bytes 8519680 | tf_op jit(solution)/shard_map/reduce_scatter | solution.py:54
  206.6 1.6 copy-start.2
Sparse Core Ops, SparseCore 0:
  9.9 112.6 all-gather.2
  124.3 53.8 all-gather.4
  180.7 82.8 reduce-scatter.2
  266.2 293.8 reduce-scatter.4
where the time goes:
time: 573 us; the launch traced here: 569 us
  waiting for transfers between devices  470 us (82%)
  local copies, waits for them, and re-layouts  29.6 us (5%)
  matrix products  27.3 us (5%)
  blocking collectives  17.4 us (3%)
  between operations  14.5 us (3%)
  other arithmetic  10.4 us (2%)
    reduce_scatter x1, waiting for transfers between devices, local(): lax.psum_scatter(jnp.where(occupied[:, None, None], jnp.take(grad_pairs,...  294 us
    all_gather x1, waiting for transfers between devices, local(): lax.all_gather(tile_values, 'fsdp', axis=1, tiled=True)  93 us
    all_gather x1, waiting for transfers between devices, local(): full_cotangent = lax.all_gather(cotangent, 'tensor', axis=1, tiled=True)  40.5 us
    reduce_scatter x1, waiting for transfers between devices, local(): lax.psum_scatter(partial_value, 'tensor', scatter_dimension=1, tiled=True)  40.5 us
    unnamed x1, blocking collectives  17.4 us
    unnamed x14, local copies, waits for them, and re-layouts  15.8 us
  transfers between devices with their start and end apart: 4, of which 4 were waited for; matrix products, arithmetic and copies ran while one was open for 11% of the time, Pallas kernels for 0%

commit v1 on v0

v1 whole, which is shorter than its diff:
```python
import functools

import jax
import jax.numpy as jnp
from jax import lax
from jax.experimental import pallas as pl
from jax.experimental.pallas import tpu as pltpu
from jax.sharding import PartitionSpec as P

MESH = pl.DeviceIdType.MESH
TILE = 128
RING = 4


def rem(value, by):
    return lax.rem(value, jnp.int32(by))


def div(value, by):
    return lax.div(value, jnp.int32(by))


def rows(start, size, unit=16):
    return pl.ds(pl.multiple_of(start, unit), size)


def kernel(
    norm_hbm, cot_hbm, tiles_hbm, places_hbm, values_ref, gi_hbm, update_ref,
    norm, cot, cot_t, tiles, places, table, table_s, weight, part, z1, z2, grad, packed, core_in,
    b1, b2, a1, a2, zl_in, gi, local_sem, send_sem, recv_sem,
):
    tokens, features = norm.shape
    half = tokens // 2
    f, t = lax.axis_index("fsdp"), lax.axis_index("tensor")
    core, y, x, zl = rem(f, 2), rem(div(f, 2), 4), rem(div(f, 8), 4), div(f, 32)
    a = x + core * (y - x)
    b = y + core * (x - y)
    step_a, step_b = 8 - 6 * core, 2 + 6 * core

    def at(aa, bb, zz):
        return (zz * 32 + aa * step_a + bb * step_b + core, t)

    def near(i, by):
        return rem(i + by + RING, RING)

    right, left = (f, near(t, 1)), (f, near(t, -1))
    up_a, down_a = at(near(a, 1), b, zl), at(near(a, -1), b, zl)
    up_b, down_b = at(a, near(b, 1), zl), at(a, near(b, -1), zl)
    other_zl = at(a, b, 1 - zl)
    other_core = (f + 1 - 2 * core, t)

    count = [0]
    started = []

    def send(src, dst, to):
        i = count[0]
        count[0] += 1
        copy = pltpu.make_async_remote_copy(
            src_ref=src, dst_ref=dst, send_sem=send_sem.at[i], recv_sem=recv_sem.at[i],
            device_id=to, device_id_type=MESH,
        )
        started.append(copy)
        return copy

    get_norm = pltpu.make_async_copy(norm_hbm, norm, local_sem.at[0])
    get_norm.start()
    get_cot = pltpu.make_async_copy(cot_hbm, cot.at[t], local_sem.at[1])
    get_cot.start()
    mine = ((core * RING + b) * RING + a) * 2 + zl
    get_tiles = pltpu.make_async_copy(tiles_hbm, tiles.at[pl.ds(mine * 2, 2)], local_sem.at[2])
    get_tiles.start()
    get_places = pltpu.make_async_copy(places_hbm, places.at[pl.ds(mine, 1)], local_sem.at[5])
    get_places.start()

    barrier = pltpu.get_barrier_semaphore()
    partners = (right, left, up_a, down_a, up_b, down_b, other_zl, other_core)
    for partner in partners:
        pl.semaphore_signal(barrier, inc=1, device_id=partner, device_id_type=MESH)
    pl.semaphore_wait(barrier, len(partners))

    first = (
        send(tiles_hbm, tiles.at[pl.ds(mine * 2, 2)], other_zl),
        send(places_hbm, places.at[pl.ds(mine, 1)], other_zl),
    )
    for copy in first:
        copy.start()
    low, high = pl.ds(0, half), pl.ds(half, half)
    cot_r = [send(cot_hbm.at[h], cot.at[t, h], right) for h in (low, high)]
    cot_l = [send(cot_hbm.at[h], cot.at[t, h], left) for h in (high, low)]
    for i in range(2):
        cot_r[i].start()
        cot_l[i].start()
    get_tiles.wait()
    get_places.wait()
    for copy in first:
        copy.wait_recv()

    def send_owners(start, size, to):
        pieces = tiles.at[pl.ds(start * 2, size * 2)], places.at[pl.ds(start, size)]
        copies = [send(piece, piece, to) for piece in pieces]
        for copy in copies:
            copy.start()
        return copies

    def arrived(copies):
        for copy in copies:
            copy.wait_recv()

    def ring_gather(origin, size, index, up, down):
        def block(i):
            return origin + i * size

        ups = send_owners(block(index), size, up)
        downs = send_owners(block(index), size, down)
        yield
        arrived(ups)
        ups = send_owners(block(near(index, -1)), size // 2, up)
        arrived(downs)
        downs = send_owners(block(near(index, 1)) + size // 2, size // 2, down)
        yield
        arrived(ups)
        arrived(downs)
        yield

    for _ in ring_gather((core * RING + b) * 8, 2, a, up_a, down_a):
        pass

    def to_core(i):
        return send_owners((core * RING + i) * 8, 8, other_core)

    second = ring_gather(core * RING * 8, 8, b, up_b, down_b)
    next(second)
    across = to_core(b)
    cot_r[0].wait_recv()
    left_t, right_t = near(t, -1), near(t, 1)
    pass_r = send(cot.at[left_t, low], cot.at[left_t, low], right)
    pass_r.start()
    cot_l[0].wait_recv()
    pass_l = send(cot.at[right_t, high], cot.at[right_t, high], left)
    pass_l.start()
    next(second)
    across += to_core(near(b, -1)) + to_core(near(b, 1))
    next(second)
    across += to_core(near(b, 2))
    arrived(across)

    lane = lax.broadcasted_iota(jnp.int32, (8, TILE), 1)
    slot = lax.broadcasted_iota(jnp.int32, (8, TILE), 0) // 4

    def place(d, sums):
        pair = places[d]
        where_is = jnp.where(pair == lane, d * 2 + slot + 1, 0)
        pair_of = jnp.where(lane == d * 2 + slot, pair, 0)
        return jnp.maximum(sums[0], where_is), sums[1] + pair_of

    zero = jnp.zeros((8, TILE), jnp.int32)
    where_is, pair_of = lax.fori_loop(0, 64, place, (zero, zero))
    table[0:8, :] = where_is
    table[8:16, :] = pair_of
    get_table = pltpu.make_async_copy(table, table_s, local_sem.at[3])
    get_table.start()
    get_table.wait()

    def assemble(r, _):
        for c in range(8):
            code = jnp.maximum(table_s[0, r * 8 + c], table_s[4, r * 8 + c])
            tile = tiles[jnp.maximum(code, 1) - 1]
            tile = jnp.where(code > 0, tile, jnp.zeros_like(tile))
            weight[c // 2, rows(r * TILE, TILE, TILE), (c % 2) * TILE : (c % 2 + 1) * TILE] = tile
        return 0

    lax.fori_loop(0, features // TILE, assemble, 0)
    get_norm.wait()

    def partial(rel, h):
        at_rows = rows(h * half, half, half)
        part[rel, at_rows, :] = jnp.dot(
            norm[at_rows, :], weight[rem(t + rel, RING)], preferred_element_type=jnp.float32
        )

    r1 = send(part.at[2, low], z1.at[0], right)
    l1 = send(part.at[2, high], z1.at[1], left)
    r2 = send(part.at[1, high], z2.at[0, high], right)
    l2 = send(part.at[3, low], z2.at[1, low], left)

    def opposite(h, _):
        partial(2, h)
        pl.when(h == 0)(r1.start)
        pl.when(h == 1)(l1.start)
        return 0

    lax.fori_loop(0, 2, opposite, 0)

    def alone(i, _):
        partial(1 + 2 * i, 1 - i)
        pl.when(i == 0)(r2.start)
        pl.when(i == 1)(l2.start)
        return 0

    lax.fori_loop(0, 2, alone, 0)

    def joined(i, _):
        partial(1 + 2 * i, i)
        return 0

    lax.fori_loop(0, 2, joined, 0)

    def own(h, _):
        partial(0, h)
        return 0

    lax.fori_loop(0, 2, own, 0)

    get_cot.wait()
    cot_r[1].wait_recv()
    cot_l[1].wait_recv()
    pass_r.wait_recv()
    pass_l.wait_recv()
    width = cot.shape[2]
    for q in range(RING):
        cot_t[q * width : (q + 1) * width, :] = cot[q].T

    def gradient(n, _):
        block, side = div(n, 2), rem(n, 2)
        out = jnp.dot(
            cot_t[rows(side * 512, 512, 512), :],
            norm[:, rows(block * 256, 256, 256)],
            preferred_element_type=jnp.float32,
        )
        for i in range(2):
            for j in range(4):
                grad[(block * 2 + i) * 8 + side * 4 + j] = out[
                    j * TILE : (j + 1) * TILE, i * TILE : (i + 1) * TILE
                ]
        return 0

    lax.fori_loop(0, features // 128, gradient, 0)

    def pack(side, whose, i):
        def one(s, _):
            slot = i * 16 + s
            pair = table_s[8, whose * 64 + slot] + table_s[12, whose * 64 + slot]
            tile = grad[jnp.maximum(pair, 0)]
            packed[side, slot] = jnp.where(pair >= 0, tile, jnp.zeros_like(tile))
            return 0

        lax.fori_loop(0, 16, one, 0)

    core_copies = []
    for i in range(RING):
        pack(1, 1 - core, i)
        piece = pl.ds(i * 16, 16)
        copy = send(packed.at[1, piece], core_in.at[piece], other_core)
        copy.start()
        core_copies.append(copy)
    for i in range(RING):
        pack(0, core, i)

    def input_block(n, _):
        th, block = div(n, 8), rem(n, 8)
        at_rows = rows(th * half, half, half)
        at_cols = rows(block * 256, 256, 256)
        lhs = jnp.concatenate([cot[q, at_rows, :] for q in range(RING)], axis=1)
        rhs = jnp.concatenate([weight[q, at_cols, :] for q in range(RING)], axis=1)
        out = lax.dot_general(lhs, rhs, (((1,), (1,)), ((), ())), preferred_element_type=jnp.float32)
        gi[at_rows, at_cols] = out.astype(jnp.bfloat16)
        return 0

    lax.fori_loop(0, 16, input_block, 0)
    put_gi = pltpu.make_async_copy(gi, gi_hbm, local_sem.at[4])
    put_gi.start()

    for copy in core_copies:
        copy.wait_recv()

    def add_core(s, _):
        packed[0, s] = packed[0, s] + core_in[s]
        return 0

    lax.fori_loop(0, 64, add_core, 0)

    def add_into(dst, dst_at, src, src_at, size):
        def one(s, _):
            dst[dst_at + s] = dst[dst_at + s] + src[src_at + s]
            return 0

        lax.fori_loop(0, size, one, 0)

    acc = packed.at[0]

    def ring_scatter(size, origin, index, up, down, in1, in2):
        part_size = size // 2

        def block(i):
            return origin + i * size

        far = block(near(index, 2))
        above, below = block(near(index, 1)), block(near(index, -1))
        firsts, lasts = pl.ds(0, part_size), pl.ds(part_size, part_size)
        u1 = send(acc.at[pl.ds(far, part_size)], in1.at[firsts], up)
        d1 = send(acc.at[pl.ds(far + part_size, part_size)], in1.at[lasts], down)
        u1.start()
        d1.start()
        u2 = send(acc.at[pl.ds(above + part_size, part_size)], in2.at[0, lasts], up)
        d2 = send(acc.at[pl.ds(below, part_size)], in2.at[1, firsts], down)
        u2.start()
        d2.start()
        yield
        u1.wait_recv()
        add_into(acc, above, in1, 0, part_size)
        u3 = send(acc.at[pl.ds(above, part_size)], in2.at[0, firsts], up)
        u3.start()
        d1.wait_recv()
        add_into(acc, below + part_size, in1, part_size, part_size)
        d3 = send(acc.at[pl.ds(below + part_size, part_size)], in2.at[1, lasts], down)
        d3.start()
        yield
        for copy in (u2, d2, u3, d3):
            copy.wait_recv()
        keep = block(index)

        def one(s, _):
            acc[keep + s] = acc[keep + s] + in2[0, s] + in2[1, s]
            return 0

        lax.fori_loop(0, size, one, 0)
        yield

    over_b = ring_scatter(16, 0, b, up_b, down_b, b1, b2)
    next(over_b)

    quarter = half // 2
    lasts_r, lasts_l = [], []
    r1.wait_recv()
    for i in range(2):
        piece = pl.ds(i * quarter, quarter)
        part[1, piece, :] = part[1, piece, :] + z1[0, piece, :]
        copy = send(part.at[1, piece], z2.at[0, piece], right)
        copy.start()
        lasts_r.append(copy)
    l1.wait_recv()
    for i in range(2):
        piece = pl.ds(half + i * quarter, quarter)
        part[3, piece, :] = part[3, piece, :] + z1[1, pl.ds(i * quarter, quarter), :]
        copy = send(part.at[3, piece], z2.at[1, piece], left)
        copy.start()
        lasts_l.append(copy)

    next(over_b)
    next(over_b)
    over_a = ring_scatter(4, b * 16, a, up_a, down_a, a1, a2)
    for _ in over_a:
        pass
    kept = b * 16 + a * 4
    zl_copy = send(acc.at[pl.ds(kept + 2 * (1 - zl), 2)], zl_in, other_zl)
    zl_copy.start()

    def finish(i):
        piece = pl.ds(i * quarter, quarter)
        values_ref[piece, :] = (part[0, piece, :] + z2[0, piece, :] + z2[1, piece, :]).astype(jnp.bfloat16)

    zl_copy.wait_recv()
    for k in range(2):
        tile = acc[kept + 2 * zl + k] + zl_in[k]
        mean = jnp.sum(tile * tile, axis=(0, 1), keepdims=True) / (TILE * TILE)
        update_ref[k] = (tile * lax.rsqrt(mean + 1e-06)).T.astype(jnp.bfloat16)

    r2.wait_recv()
    l2.wait_recv()
    for i in range(2):
        lasts_r[i].wait_recv()
        finish(i)
        lasts_l[i].wait_recv()
        finish(2 + i)
    put_gi.wait()
    for copy in started:
        copy.wait_send()


COPIES = 57


def local(normed, tile_values, tile_rows, tile_columns, cotangent):
    tokens, features = normed.shape
    width = cotangent.shape[1]
    pair = jnp.where(tile_columns >= 0, tile_rows * 8 + tile_columns, -1)
    places = jnp.broadcast_to(pair.reshape(2, 1, 1), (2, 4, TILE)).reshape(1, 8, TILE)
    anywhere = pl.BlockSpec(memory_space=pl.ANY)
    vmem = pl.BlockSpec(memory_space=pltpu.VMEM)
    f32, bf16 = jnp.float32, jnp.bfloat16
    values, grad_input, update = pl.pallas_call(
        kernel,
        out_shape=(
            jax.ShapeDtypeStruct((tokens, width), bf16),
            jax.ShapeDtypeStruct((tokens, features), bf16),
            jax.ShapeDtypeStruct((2, TILE, TILE), bf16),
        ),
        in_specs=[anywhere] * 4,
        out_specs=(vmem, anywhere, vmem),
        scratch_shapes=[
            pltpu.VMEM((tokens, features), bf16),
            pltpu.VMEM((RING, tokens, width), bf16),
            pltpu.VMEM((RING * width, tokens), bf16),
            pltpu.VMEM((128, TILE, TILE), bf16),
            pltpu.VMEM((64, 8, TILE), jnp.int32),
            pltpu.VMEM((16, TILE), jnp.int32),
            pltpu.SMEM((16, TILE), jnp.int32),
            pltpu.VMEM((RING, features, width), bf16),
            pltpu.VMEM((RING, tokens, width), f32),
            pltpu.VMEM((2, tokens // 2, width), f32),
            pltpu.VMEM((2, tokens, width), f32),
            pltpu.VMEM((128, TILE, TILE), f32),
            pltpu.VMEM((2, 64, TILE, TILE), f32),
            pltpu.VMEM((64, TILE, TILE), f32),
            pltpu.VMEM((16, TILE, TILE), f32),
            pltpu.VMEM((2, 16, TILE, TILE), f32),
            pltpu.VMEM((4, TILE, TILE), f32),
            pltpu.VMEM((2, 4, TILE, TILE), f32),
            pltpu.VMEM((2, TILE, TILE), f32),
            pltpu.VMEM((tokens, features), bf16),
            pltpu.SemaphoreType.DMA((6,)),
            pltpu.SemaphoreType.DMA((COPIES,)),
            pltpu.SemaphoreType.DMA((COPIES,)),
        ],
        compiler_params=pltpu.CompilerParams(
            collective_id=0, has_side_effects=True, vmem_limit_bytes=67043328
        ),
    )(normed, cotangent, tile_values.reshape(2, TILE, TILE), places)
    return values, grad_input, update[None]


def solution(mesh):
    in_specs = (
        P("fsdp", "tensor"),
        P("tensor", "fsdp", None, None),
        P("tensor", "fsdp"),
        P("tensor", "fsdp"),
        P("fsdp", "tensor"),
    )
    out_specs = (P("fsdp", "tensor"), P("fsdp", "tensor"), P("tensor", "fsdp", None, None))
    return jax.shard_map(local, mesh=mesh, in_specs=in_specs, out_specs=out_specs, check_vma=False)
```

time: 573 us -> 137 us (0.24)
  the two profiles are of different devices: /device:TPU:1 before, /device:TPU:64 now
where the time goes in v1:
time: 137 us
  Pallas kernels  128 us (93%)
  local copies, waits for them, and re-layouts  8.14 us (6%)
    pallas_call x1, Pallas kernels, local(): pl.pallas_call(kernel, out_shape=(jax.ShapeDtypeStruct((tokens, width), b...  128 us
    unnamed x5, local copies, waits for them, and re-layouts  7.32 us

profile of v1, /device:TPU:64, one launch (start us, length us, event | category | flops | bytes accessed | tf_op | source)
XLA Modules:
  0.0 137.0 jit_solution(3488438836419976072)
XLA Ops:
  0.6 0.7 fusion
  1.3 0.1 broadcast_in_dim.20
  1.4 0.1 broadcast_in_dim.21
  1.5 0.7 broadcast_in_dim.22.places_hbm
  2.1 127.6 %shard_map.76 = (bf16[1024,256]{1,0:T(8,128)(2,1)}, bf16[1024,2048]{1,0:T(8,128)(2,1)}, bf16[2,128,128]{2,1,0:T(8,128)(2,1)}) custom-call(bf16[1024,2048]{1,0:T(8,128)(2,1)} %norm_hbm.1, bf16[1024,256]{1,0:T(8,128)(2,1)} %cot_hbm.1, bf16[2,128,128]{2,1,0:T(8,128)(2,1)} %bitcast.4, s32[1,8,128]{2,1,0:T(8,128)} %broadcast_in_dim.22.places_hbm), custom_call_target="tpu_custom_call" | custom-call | tf_op jit(solution)/shard_map/pallas_call | solution.py:391
  129.7 1.9 %copy.11 = bf16[1024,256]{1,0:T(8,128)(2,1)} copy(bf16[1024,256]{1,0:T(8,128)(2,1)} %get-tuple-element.12) | data formatting | bytes 1048576
  131.6 0.0 copy-start
  131.6 4.8 %copy.12 = bf16[1024,2048]{1,0:T(8,128)(2,1)} copy(bf16[1024,2048]{1,0:T(8,128)(2,1)} %get-tuple-element.13) | data formatting | bytes 8388608
  136.4 0.0 copy-done
  136.4 0.6 copy.13
Async XLA Ops:
  131.6 4.8 %copy-start = (bf16[2,128,128]{2,1,0:T(8,128)(2,1)S(1)}, bf16[2,128,128]{2,1,0:T(8,128)(2,1)}, u32[]{:S(2)}) copy-start(bf16[2,128,128]{2,1,0:T(8,128)(2,1)} %get-tuple-element.8) | copy-start | bytes 196612

commit v2 on v1

--- a/solution.py
+++ b/solution.py
@@ -24,10 +24,30 @@
     return pl.ds(pl.multiple_of(start, unit), size)
 
 
+CODED = True
+
+
+def encode(x):
+    if not CODED:
+        return x, None
+    groups = x.reshape(8, x.shape[0] // 8, x.shape[1])
+    largest = jnp.maximum(jnp.max(jnp.abs(groups), axis=1), 1e-30)
+    whole = lax.round(groups * (32767.0 / largest)[:, None, :], lax.RoundingMethod.TO_NEAREST_EVEN)
+    return whole.astype(jnp.int32).astype(jnp.int16).reshape(x.shape), largest * (1 / 32767.0)
+
+
+def decode(coded, scales):
+    if not CODED:
+        return coded
+    groups = coded.astype(jnp.int32).astype(jnp.float32).reshape(8, coded.shape[0] // 8, coded.shape[1])
+    return (groups * scales[:, None, :]).reshape(coded.shape)
+
+
 def kernel(
     norm_hbm, cot_hbm, tiles_hbm, places_hbm, values_ref, gi_hbm, update_ref,
-    norm, cot, cot_t, tiles, places, table, table_s, weight, part, z1, z2, grad, packed, core_in,
-    b1, b2, a1, a2, zl_in, gi, local_sem, send_sem, recv_sem,
+    norm, cot, cot_t, tiles, places, table, table_s, weight, own, joint, z_out, z_in, s_out, s_in,
+    grad, packed, core_in, b1, b2, a1, a2, zl_in, gi, local_sem, send_sem, recv_sem,
+    z_send, z_recv, s_send, s_recv,
 ):
     tokens, features = norm.shape
     half = tokens // 2
@@ -87,13 +107,13 @@
     low, high = pl.ds(0, half), pl.ds(half, half)
     cot_r = [send(cot_hbm.at[h], cot.at[t, h], right) for h in (low, high)]
     cot_l = [send(cot_hbm.at[h], cot.at[t, h], left) for h in (high, low)]
+    for copy in first:
+        copy.wait_recv()
     for i in range(2):
         cot_r[i].start()
         cot_l[i].start()
     get_tiles.wait()
     get_places.wait()
-    for copy in first:
-        copy.wait_recv()
 
     def send_owners(start, size, to):
         pieces = tiles.at[pl.ds(start * 2, size * 2)], places.at[pl.ds(start, size)]
@@ -122,26 +142,56 @@
         arrived(downs)
         yield
 
-    for _ in ring_gather((core * RING + b) * 8, 2, a, up_a, down_a):
-        pass
-
     def to_core(i):
         return send_owners((core * RING + i) * 8, 8, other_core)
 
-    second = ring_gather(core * RING * 8, 8, b, up_b, down_b)
-    next(second)
+    def turn(q):
+        cot_t[q] = cot[q].T
+
+    def gradient(q, start, stop):
+        def one(n, _):
+            out = jnp.dot(
+                cot_t[q], norm[:, rows(n * 256, 256, 256)], preferred_element_type=jnp.float32
+            )
+            for i in range(2):
+                for j in range(2):
+                    grad[(n * 2 + i) * 8 + q * 2 + j] = out[
+                        j * TILE : (j + 1) * TILE, i * TILE : (i + 1) * TILE
+                    ]
+            return 0
+
+        lax.fori_loop(start, stop, one, 0)
+
+    steps = features // 256
+    left_t, right_t, far_t = near(t, -1), near(t, 1), near(t, 2)
+    first_ring = ring_gather((core * RING + b) * 8, 2, a, up_a, down_a)
+    next(first_ring)
+    get_cot.wait()
+    turn(t)
+    next(first_ring)
+    get_norm.wait()
+    gradient(t, 0, steps // 4)
+    next(first_ring)
+    second_ring = ring_gather(core * RING * 8, 8, b, up_b, down_b)
+    next(second_ring)
     across = to_core(b)
+    gradient(t, steps // 4, steps)
     cot_r[0].wait_recv()
-    left_t, right_t = near(t, -1), near(t, 1)
     pass_r = send(cot.at[left_t, low], cot.at[left_t, low], right)
     pass_r.start()
     cot_l[0].wait_recv()
     pass_l = send(cot.at[right_t, high], cot.at[right_t, high], left)
     pass_l.start()
-    next(second)
+    next(second_ring)
     across += to_core(near(b, -1)) + to_core(near(b, 1))
-    next(second)
+    next(second_ring)
     across += to_core(near(b, 2))
+    cot_r[1].wait_recv()
+    turn(left_t)
+    gradient(left_t, 0, steps)
+    cot_l[1].wait_recv()
+    turn(right_t)
+    gradient(right_t, 0, steps)
     arrived(across)
 
     lane = lax.broadcasted_iota(jnp.int32, (8, TILE), 1)
@@ -157,7 +207,7 @@
     where_is, pair_of = lax.fori_loop(0, 64, place, (zero, zero))
     table[0:8, :] = where_is
     table[8:16, :] = pair_of
-    get_table = pltpu.make_async_copy(table, table_s, local_sem.at[3])
+    get_table = pltpu.make_async_copy(table, table_s, local_sem.at[6])
     get_table.start()
     get_table.wait()
 
@@ -170,71 +220,61 @@
         return 0
 
     lax.fori_loop(0, features // TILE, assemble, 0)
-    get_norm.wait()
-
-    def partial(rel, h):
-        at_rows = rows(h * half, half, half)
-        part[rel, at_rows, :] = jnp.dot(
-            norm[at_rows, :], weight[rem(t + rel, RING)], preferred_element_type=jnp.float32
-        )
-
-    r1 = send(part.at[2, low], z1.at[0], right)
-    l1 = send(part.at[2, high], z1.at[1], left)
-    r2 = send(part.at[1, high], z2.at[0, high], right)
-    l2 = send(part.at[3, low], z2.at[1, low], left)
-
-    def opposite(h, _):
-        partial(2, h)
-        pl.when(h == 0)(r1.start)
-        pl.when(h == 1)(l1.start)
-        return 0
-
-    lax.fori_loop(0, 2, opposite, 0)
-
-    def alone(i, _):
-        partial(1 + 2 * i, 1 - i)
-        pl.when(i == 0)(r2.start)
-        pl.when(i == 1)(l2.start)
-        return 0
-
-    lax.fori_loop(0, 2, alone, 0)
-
-    def joined(i, _):
-        partial(1 + 2 * i, i)
-        return 0
-
-    lax.fori_loop(0, 2, joined, 0)
-
-    def own(h, _):
-        partial(0, h)
-        return 0
-
-    lax.fori_loop(0, 2, own, 0)
-
-    get_cot.wait()
-    cot_r[1].wait_recv()
-    cot_l[1].wait_recv()
-    pass_r.wait_recv()
-    pass_l.wait_recv()
-    width = cot.shape[2]
-    for q in range(RING):
-        cot_t[q * width : (q + 1) * width, :] = cot[q].T
-
-    def gradient(n, _):
-        block, side = div(n, 2), rem(n, 2)
-        out = jnp.dot(
-            cot_t[rows(side * 512, 512, 512), :],
-            norm[:, rows(block * 256, 256, 256)],
+
+    chunk = tokens // 4
+
+    def partial(rel, c):
+        return jnp.dot(
+            norm[rows(c * chunk, chunk, chunk), :],
+            weight[rem(t + rel, RING)],
             preferred_element_type=jnp.float32,
         )
-        for i in range(2):
-            for j in range(4):
-                grad[(block * 2 + i) * 8 + side * 4 + j] = out[
-                    j * TILE : (j + 1) * TILE, i * TILE : (i + 1) * TILE
-                ]
-        return 0
-
-    lax.fori_loop(0, features // 128, gradient, 0)
+
+    def message(way, j):
+        to = (f, rem(t + 1 + 2 * way, RING))
+        copies = [
+            pltpu.make_async_remote_copy(
+                src_ref=z_out.at[way, j], dst_ref=z_in.at[way, j], send_sem=z_send.at[way, j],
+                recv_sem=z_recv.at[way, j], device_id=to, device_id_type=MESH,
+            )
+        ]
+        if CODED:
+            copies += [
+                pltpu.make_async_remote_copy(
+                    src_ref=s_out.at[way, j], dst_ref=s_in.at[way, j], send_sem=s_send.at[way, j],
+                    recv_sem=s_recv.at[way, j], device_id=to, device_id_type=MESH,
+                )
+            ]
+        return copies
+
+    def post(way, j, x):
+        coded, scales = encode(x)
+        z_out[way, j] = coded
+        if CODED:
+            s_out[way, j] = scales
+        for copy in message(way, j):
+            copy.start()
+
+    def received(way, j):
+        return decode(z_in[way, j], s_in[way, j])
+
+    def to_far(i, _):
+        way, j = div(i, 2), rem(i, 2)
+        post(way, j, partial(2, i))
+        return 0
+
+    lax.fori_loop(0, 4, to_far, 0)
+
+    def to_near(i, _):
+        way, j = div(i, 2), rem(i, 2)
+        post(way, 2 + j, partial(1 + 2 * way, (1 - way) * 2 + j))
+        return 0
+
+    lax.fori_loop(0, 4, to_near, 0)
+
+    arrived([pass_r, pass_l])
+    turn(far_t)
+    gradient(far_t, 0, steps)
 
     def pack(side, whose, i):
         def one(s, _):
@@ -247,7 +287,8 @@
         lax.fori_loop(0, 16, one, 0)
 
     core_copies = []
-    for i in range(RING):
+    for by in (2, 1, -1, 0):
+        i = near(a, by)
         pack(1, 1 - core, i)
         piece = pl.ds(i * 16, 16)
         copy = send(packed.at[1, piece], core_in.at[piece], other_core)
@@ -255,6 +296,13 @@
         core_copies.append(copy)
     for i in range(RING):
         pack(0, core, i)
+
+    def rest(i, _):
+        joint[i] = partial(1 + 2 * div(i, 2), i)
+        own[i] = partial(0, i)
+        return 0
+
+    lax.fori_loop(0, 4, rest, 0)
 
     def input_block(n, _):
         th, block = div(n, 8), rem(n, 8)
@@ -266,18 +314,12 @@
         gi[at_rows, at_cols] = out.astype(jnp.bfloat16)
         return 0
 
-    lax.fori_loop(0, 16, input_block, 0)
-    put_gi = pltpu.make_async_copy(gi, gi_hbm, local_sem.at[4])
-    put_gi.start()
-
-    for copy in core_copies:
-        copy.wait_recv()
-
-    def add_core(s, _):
-        packed[0, s] = packed[0, s] + core_in[s]
-        return 0
-
-    lax.fori_loop(0, 64, add_core, 0)
+    def grad_input(th):
+        lax.fori_loop(th * 8, th * 8 + 8, input_block, 0)
+        at_rows = pl.ds(th * half, half)
+        put = pltpu.make_async_copy(gi.at[at_rows], gi_hbm.at[at_rows], local_sem.at[3 + th])
+        put.start()
+        return put
 
     def add_into(dst, dst_at, src, src_at, size):
         def one(s, _):
@@ -288,7 +330,7 @@
 
     acc = packed.at[0]
 
-    def ring_scatter(size, origin, index, up, down, in1, in2):
+    def ring_scatter(size, origin, index, up, down, in1, in2, before):
         part_size = size // 2
 
         def block(i):
@@ -297,14 +339,18 @@
         far = block(near(index, 2))
         above, below = block(near(index, 1)), block(near(index, -1))
         firsts, lasts = pl.ds(0, part_size), pl.ds(part_size, part_size)
+        before(2)
         u1 = send(acc.at[pl.ds(far, part_size)], in1.at[firsts], up)
         d1 = send(acc.at[pl.ds(far + part_size, part_size)], in1.at[lasts], down)
         u1.start()
         d1.start()
+        before(1)
+        before(-1)
         u2 = send(acc.at[pl.ds(above + part_size, part_size)], in2.at[0, lasts], up)
         d2 = send(acc.at[pl.ds(below, part_size)], in2.at[1, firsts], down)
         u2.start()
         d2.start()
+        before(0)
         yield
         u1.wait_recv()
         add_into(acc, above, in1, 0, part_size)
@@ -326,58 +372,58 @@
         lax.fori_loop(0, size, one, 0)
         yield
 
-    over_b = ring_scatter(16, 0, b, up_b, down_b, b1, b2)
+    def add_core(by):
+        core_copies[(2, 1, -1, 0).index(by)].wait_recv()
+        start = near(b, by) * 16
+        add_into(acc, start, core_in, start, 16)
+
+    over_b = ring_scatter(16, 0, b, up_b, down_b, b1, b2, add_core)
     next(over_b)
 
-    quarter = half // 2
-    lasts_r, lasts_l = [], []
-    r1.wait_recv()
-    for i in range(2):
-        piece = pl.ds(i * quarter, quarter)
-        part[1, piece, :] = part[1, piece, :] + z1[0, piece, :]
-        copy = send(part.at[1, piece], z2.at[0, piece], right)
-        copy.start()
-        lasts_r.append(copy)
-    l1.wait_recv()
-    for i in range(2):
-        piece = pl.ds(half + i * quarter, quarter)
-        part[3, piece, :] = part[3, piece, :] + z1[1, pl.ds(i * quarter, quarter), :]
-        copy = send(part.at[3, piece], z2.at[1, piece], left)
-        copy.start()
-        lasts_l.append(copy)
-
+    def pass_on(i, _):
+        way, j = div(i, 2), rem(i, 2)
+        for copy in message(way, j):
+            copy.wait_recv()
+        post(way, 4 + j, joint[i] + received(way, j))
+        return 0
+
+    lax.fori_loop(0, 4, pass_on, 0)
+    puts = [grad_input(0)]
     next(over_b)
+    puts += [grad_input(1)]
     next(over_b)
-    over_a = ring_scatter(4, b * 16, a, up_a, down_a, a1, a2)
-    for _ in over_a:
+    for _ in ring_scatter(4, b * 16, a, up_a, down_a, a1, a2, lambda by: None):
         pass
     kept = b * 16 + a * 4
     zl_copy = send(acc.at[pl.ds(kept + 2 * (1 - zl), 2)], zl_in, other_zl)
     zl_copy.start()
 
-    def finish(i):
-        piece = pl.ds(i * quarter, quarter)
-        values_ref[piece, :] = (part[0, piece, :] + z2[0, piece, :] + z2[1, piece, :]).astype(jnp.bfloat16)
-
+    def finish(i, _):
+        h, j = div(i, 2), rem(i, 2)
+        from_left, from_right = 4 - 2 * h + j, 2 + 2 * h + j
+        for copy in message(0, from_left) + message(1, from_right):
+            copy.wait_recv()
+        total = own[i] + received(0, from_left) + received(1, from_right)
+        values_ref[rows(i * chunk, chunk, chunk), :] = total.astype(jnp.bfloat16)
+        return 0
+
+    lax.fori_loop(0, 4, finish, 0)
     zl_copy.wait_recv()
     for k in range(2):
         tile = acc[kept + 2 * zl + k] + zl_in[k]
         mean = jnp.sum(tile * tile, axis=(0, 1), keepdims=True) / (TILE * TILE)
         update_ref[k] = (tile * lax.rsqrt(mean + 1e-06)).T.astype(jnp.bfloat16)
-
-    r2.wait_recv()
-    l2.wait_recv()
-    for i in range(2):
-        lasts_r[i].wait_recv()
-        finish(i)
-        lasts_l[i].wait_recv()
-        finish(2 + i)
-    put_gi.wait()
+    for put in puts:
+        put.wait()
     for copy in started:
         copy.wait_send()
-
-
-COPIES = 57
+    for way in range(2):
+        for j in range(6):
+            for copy in message(way, j):
+                copy.wait_send()
+
+
+COPIES = 49
 
 
 def local(normed, tile_values, tile_rows, tile_columns, cotangent):
@@ -388,6 +434,7 @@
     anywhere = pl.BlockSpec(memory_space=pl.ANY)
     vmem = pl.BlockSpec(memory_space=pltpu.VMEM)
     f32, bf16 = jnp.float32, jnp.bfloat16
+    sent = jnp.int16 if CODED else f32
     values, grad_input, update = pl.pallas_call(
         kernel,
         out_shape=(
@@ -400,15 +447,18 @@
         scratch_shapes=[
             pltpu.VMEM((tokens, features), bf16),
             pltpu.VMEM((RING, tokens, width), bf16),
-            pltpu.VMEM((RING * width, tokens), bf16),
+            pltpu.VMEM((RING, width, tokens), bf16),
             pltpu.VMEM((128, TILE, TILE), bf16),
             pltpu.VMEM((64, 8, TILE), jnp.int32),
             pltpu.VMEM((16, TILE), jnp.int32),
             pltpu.SMEM((16, TILE), jnp.int32),
             pltpu.VMEM((RING, features, width), bf16),
-            pltpu.VMEM((RING, tokens, width), f32),
-            pltpu.VMEM((2, tokens // 2, width), f32),
-            pltpu.VMEM((2, tokens, width), f32),
+            pltpu.VMEM((4, tokens // 4, width), f32),
+            pltpu.VMEM((4, tokens // 4, width), f32),
+            pltpu.VMEM((2, 6, tokens // 4, width), sent),
+            pltpu.VMEM((2, 6, tokens // 4, width), sent),
+            pltpu.VMEM((2, 6, 8, width), f32),
+            pltpu.VMEM((2, 6, 8, width), f32),
             pltpu.VMEM((128, TILE, TILE), f32),
             pltpu.VMEM((2, 64, TILE, TILE), f32),
             pltpu.VMEM((64, TILE, TILE), f32),
@@ -418,9 +468,10 @@
             pltpu.VMEM((2, 4, TILE, TILE), f32),
             pltpu.VMEM((2, TILE, TILE), f32),
             pltpu.VMEM((tokens, features), bf16),
-            pltpu.SemaphoreType.DMA((6,)),
+            pltpu.SemaphoreType.DMA((7,)),
             pltpu.SemaphoreType.DMA((COPIES,)),
             pltpu.SemaphoreType.DMA((COPIES,)),
+            *[pltpu.SemaphoreType.DMA((2, 6))] * 4,
         ],
         compiler_params=pltpu.CompilerParams(
             collective_id=0, has_side_effects=True, vmem_limit_bytes=67043328

time: 137 us -> 108 us (0.79)
  the two profiles are of different devices: /device:TPU:64 before, /device:TPU:10 now
where the time goes in v2:
time: 108 us
  Pallas kernels  98.5 us (91%)
  local copies, waits for them, and re-layouts  8.14 us (8%)
    pallas_call x1, Pallas kernels, local(): pl.pallas_call(kernel, out_shape=(jax.ShapeDtypeStruct((tokens, width), b...  98.5 us
    unnamed x5, local copies, waits for them, and re-layouts  7.32 us

profile of v2, /device:TPU:10, one launch (start us, length us, event | category | flops | bytes accessed | tf_op | source)
XLA Modules:
  0.0 108.0 jit_solution(6879324619668098288)
XLA Ops:
  0.6 0.7 fusion
  1.3 0.1 broadcast_in_dim.20
  1.4 0.1 broadcast_in_dim.21
  1.5 0.7 broadcast_in_dim.22.places_hbm
  2.1 98.5 %shard_map.76 = (bf16[1024,256]{1,0:T(8,128)(2,1)}, bf16[1024,2048]{1,0:T(8,128)(2,1)}, bf16[2,128,128]{2,1,0:T(8,128)(2,1)}) custom-call(bf16[1024,2048]{1,0:T(8,128)(2,1)} %norm_hbm.1, bf16[1024,256]{1,0:T(8,128)(2,1)} %cot_hbm.1, bf16[2,128,128]{2,1,0:T(8,128)(2,1)} %bitcast.4, s32[1,8,128]{2,1,0:T(8,128)} %broadcast_in_dim.22.places_hbm), custom_call_target="tpu_custom_call" | custom-call | tf_op jit(solution)/shard_map/pallas_call | solution.py:438
  100.7 1.9 %copy.11 = bf16[1024,256]{1,0:T(8,128)(2,1)} copy(bf16[1024,256]{1,0:T(8,128)(2,1)} %get-tuple-element.12) | data formatting | bytes 1048576
  102.5 0.0 copy-start
  102.5 4.8 %copy.12 = bf16[1024,2048]{1,0:T(8,128)(2,1)} copy(bf16[1024,2048]{1,0:T(8,128)(2,1)} %get-tuple-element.13) | data formatting | bytes 8388608
  107.4 0.0 copy-done
  107.4 0.6 copy.13
Async XLA Ops:
  102.5 4.8 %copy-start = (bf16[2,128,128]{2,1,0:T(8,128)(2,1)S(1)}, bf16[2,128,128]{2,1,0:T(8,128)(2,1)}, u32[]{:S(2)}) copy-start(bf16[2,128,128]{2,1,0:T(8,128)(2,1)} %get-tuple-element.8) | copy-start | bytes 196612

commit v3 on v2

--- a/solution.py
+++ b/solution.py
@@ -24,12 +24,7 @@
     return pl.ds(pl.multiple_of(start, unit), size)
 
 
-CODED = True
-
-
 def encode(x):
-    if not CODED:
-        return x, None
     groups = x.reshape(8, x.shape[0] // 8, x.shape[1])
     largest = jnp.maximum(jnp.max(jnp.abs(groups), axis=1), 1e-30)
     whole = lax.round(groups * (32767.0 / largest)[:, None, :], lax.RoundingMethod.TO_NEAREST_EVEN)
@@ -37,16 +32,14 @@
 
 
 def decode(coded, scales):
-    if not CODED:
-        return coded
     groups = coded.astype(jnp.int32).astype(jnp.float32).reshape(8, coded.shape[0] // 8, coded.shape[1])
     return (groups * scales[:, None, :]).reshape(coded.shape)
 
 
 def kernel(
-    norm_hbm, cot_hbm, tiles_hbm, places_hbm, values_ref, gi_hbm, update_ref,
+    norm_hbm, cot_hbm, tiles_hbm, rows_ref, columns_ref, values_ref, gi_hbm, update_ref,
     norm, cot, cot_t, tiles, places, table, table_s, weight, own, joint, z_out, z_in, s_out, s_in,
-    grad, packed, core_in, b1, b2, a1, a2, zl_in, gi, local_sem, send_sem, recv_sem,
+    grad, packed, core_in, bq_out, bq_in, br_out, br_in, aq_out, aq_in, ar_out, ar_in, zl_in, gi, local_sem, send_sem, recv_sem,
     z_send, z_recv, s_send, s_recv,
 ):
     tokens, features = norm.shape
@@ -89,8 +82,12 @@
     mine = ((core * RING + b) * RING + a) * 2 + zl
     get_tiles = pltpu.make_async_copy(tiles_hbm, tiles.at[pl.ds(mine * 2, 2)], local_sem.at[2])
     get_tiles.start()
-    get_places = pltpu.make_async_copy(places_hbm, places.at[pl.ds(mine, 1)], local_sem.at[5])
-    get_places.start()
+    pairs = [
+        jnp.where(columns_ref[0, k] >= 0, rows_ref[0, k] * 8 + columns_ref[0, k], -1) for k in range(2)
+    ]
+    lane = lax.broadcasted_iota(jnp.int32, (8, TILE), 1)
+    slot = lax.broadcasted_iota(jnp.int32, (8, TILE), 0) // 4
+    places[mine] = jnp.where(slot == 0, pairs[0], pairs[1])
 
     barrier = pltpu.get_barrier_semaphore()
     partners = (right, left, up_a, down_a, up_b, down_b, other_zl, other_core)
@@ -100,7 +97,7 @@
 
     first = (
         send(tiles_hbm, tiles.at[pl.ds(mine * 2, 2)], other_zl),
-        send(places_hbm, places.at[pl.ds(mine, 1)], other_zl),
+        send(places.at[mine], places.at[mine], other_zl),
     )
     for copy in first:
         copy.start()
@@ -113,7 +110,6 @@
         cot_r[i].start()
         cot_l[i].start()
     get_tiles.wait()
-    get_places.wait()
 
     def send_owners(start, size, to):
         pieces = tiles.at[pl.ds(start * 2, size * 2)], places.at[pl.ds(start, size)]
@@ -194,8 +190,6 @@
     gradient(right_t, 0, steps)
     arrived(across)
 
-    lane = lax.broadcasted_iota(jnp.int32, (8, TILE), 1)
-    slot = lax.broadcasted_iota(jnp.int32, (8, TILE), 0) // 4
 
     def place(d, sums):
         pair = places[d]
@@ -234,24 +228,17 @@
         to = (f, rem(t + 1 + 2 * way, RING))
         copies = [
             pltpu.make_async_remote_copy(
-                src_ref=z_out.at[way, j], dst_ref=z_in.at[way, j], send_sem=z_send.at[way, j],
-                recv_sem=z_recv.at[way, j], device_id=to, device_id_type=MESH,
+                src_ref=src.at[way, j], dst_ref=dst.at[way, j], send_sem=send_at.at[way, j],
+                recv_sem=recv_at.at[way, j], device_id=to, device_id_type=MESH,
+            )
+            for src, dst, send_at, recv_at in (
+                (z_out, z_in, z_send, z_recv), (s_out, s_in, s_send, s_recv)
             )
         ]
-        if CODED:
-            copies += [
-                pltpu.make_async_remote_copy(
-                    src_ref=s_out.at[way, j], dst_ref=s_in.at[way, j], send_sem=s_send.at[way, j],
-                    recv_sem=s_recv.at[way, j], device_id=to, device_id_type=MESH,
-                )
-            ]
         return copies
 
     def post(way, j, x):
-        coded, scales = encode(x)
-        z_out[way, j] = coded
-        if CODED:
-            s_out[way, j] = scales
+        z_out[way, j], s_out[way, j] = encode(x)
         for copy in message(way, j):
             copy.start()
 
@@ -264,13 +251,6 @@
         return 0
 
     lax.fori_loop(0, 4, to_far, 0)
-
-    def to_near(i, _):
-        way, j = div(i, 2), rem(i, 2)
-        post(way, 2 + j, partial(1 + 2 * way, (1 - way) * 2 + j))
-        return 0
-
-    lax.fori_loop(0, 4, to_near, 0)
 
     arrived([pass_r, pass_l])
     turn(far_t)
@@ -297,13 +277,6 @@
     for i in range(RING):
         pack(0, core, i)
 
-    def rest(i, _):
-        joint[i] = partial(1 + 2 * div(i, 2), i)
-        own[i] = partial(0, i)
-        return 0
-
-    lax.fori_loop(0, 4, rest, 0)
-
     def input_block(n, _):
         th, block = div(n, 8), rem(n, 8)
         at_rows = rows(th * half, half, half)
@@ -330,46 +303,56 @@
 
     acc = packed.at[0]
 
-    def ring_scatter(size, origin, index, up, down, in1, in2, before):
+    def ring_scatter(size, origin, index, up, down, q_out, q_in, r_out, r_in, before):
         part_size = size // 2
 
         def block(i):
             return origin + i * size
 
+        def post_slots(k, start, to, behind=None):
+            def one(s, _):
+                x = acc[start + s]
+                if behind is not None:
+                    x = x + decode(q_in[behind, s], r_in[behind, s])
+                q_out[k, s], r_out[k, s] = encode(x)
+                return 0
+
+            lax.fori_loop(0, part_size, one, 0)
+            copies = send(q_out.at[k], q_in.at[k], to), send(r_out.at[k], r_in.at[k], to)
+            for copy in copies:
+                copy.start()
+            return copies
+
         far = block(near(index, 2))
         above, below = block(near(index, 1)), block(near(index, -1))
-        firsts, lasts = pl.ds(0, part_size), pl.ds(part_size, part_size)
         before(2)
-        u1 = send(acc.at[pl.ds(far, part_size)], in1.at[firsts], up)
-        d1 = send(acc.at[pl.ds(far + part_size, part_size)], in1.at[lasts], down)
-        u1.start()
-        d1.start()
+        u1 = post_slots(0, far, up)
+        d1 = post_slots(1, far + part_size, down)
+        yield
         before(1)
+        u2 = post_slots(2, above + part_size, up)
         before(-1)
-        u2 = send(acc.at[pl.ds(above + part_size, part_size)], in2.at[0, lasts], up)
-        d2 = send(acc.at[pl.ds(below, part_size)], in2.at[1, firsts], down)
-        u2.start()
-        d2.start()
+        d2 = post_slots(3, below, down)
         before(0)
         yield
-        u1.wait_recv()
-        add_into(acc, above, in1, 0, part_size)
-        u3 = send(acc.at[pl.ds(above, part_size)], in2.at[0, firsts], up)
-        u3.start()
-        d1.wait_recv()
-        add_into(acc, below + part_size, in1, part_size, part_size)
-        d3 = send(acc.at[pl.ds(below + part_size, part_size)], in2.at[1, lasts], down)
-        d3.start()
-        yield
-        for copy in (u2, d2, u3, d3):
-            copy.wait_recv()
+        arrived(u1)
+        u3 = post_slots(4, above, up, 0)
+        arrived(d1)
+        d3 = post_slots(5, below + part_size, down, 1)
+        yield
+        arrived(u2 + d2 + u3 + d3)
         keep = block(index)
 
         def one(s, _):
-            acc[keep + s] = acc[keep + s] + in2[0, s] + in2[1, s]
+            for first_k, second_k, at_s in ((4, 3, s), (2, 5, s + part_size)):
+                acc[keep + at_s] = (
+                    acc[keep + at_s]
+                    + decode(q_in[first_k, s], r_in[first_k, s])
+                    + decode(q_in[second_k, s], r_in[second_k, s])
+                )
             return 0
 
-        lax.fori_loop(0, size, one, 0)
+        lax.fori_loop(0, part_size, one, 0)
         yield
 
     def add_core(by):
@@ -377,8 +360,25 @@
         start = near(b, by) * 16
         add_into(acc, start, core_in, start, 16)
 
-    over_b = ring_scatter(16, 0, b, up_b, down_b, b1, b2, add_core)
+    over_b = ring_scatter(16, 0, b, up_b, down_b, bq_out, bq_in, br_out, br_in, add_core)
     next(over_b)
+
+    def to_near(i, _):
+        way, j = div(i, 2), rem(i, 2)
+        post(way, 2 + j, partial(1 + 2 * way, (1 - way) * 2 + j))
+        return 0
+
+    lax.fori_loop(0, 4, to_near, 0)
+
+    next(over_b)
+
+    def rest(i, _):
+        joint[i] = partial(1 + 2 * div(i, 2), i)
+        own[i] = partial(0, i)
+        return 0
+
+    lax.fori_loop(0, 4, rest, 0)
+
 
     def pass_on(i, _):
         way, j = div(i, 2), rem(i, 2)
@@ -392,7 +392,7 @@
     next(over_b)
     puts += [grad_input(1)]
     next(over_b)
-    for _ in ring_scatter(4, b * 16, a, up_a, down_a, a1, a2, lambda by: None):
+    for _ in ring_scatter(4, b * 16, a, up_a, down_a, aq_out, aq_in, ar_out, ar_in, lambda by: None):
         pass
     kept = b * 16 + a * 4
     zl_copy = send(acc.at[pl.ds(kept + 2 * (1 - zl), 2)], zl_in, other_zl)
@@ -423,26 +423,58 @@
                 copy.wait_send()
 
 
-COPIES = 49
+COPIES = 61
+
+
+def hand_over_kernel(parts, *refs):
+    count = len(parts)
+    sources, targets, held = refs[:count], refs[count : 2 * count], refs[2 * count : 3 * count]
+    in_sem, out_sem = refs[3 * count :]
+    ins, outs = [], []
+    for source, target, hold, number in zip(sources, targets, held, parts):
+        size = source.shape[0] // number
+        for i in range(number):
+            piece, k = pl.ds(i * size, size), len(ins)
+            ins.append(pltpu.make_async_copy(source.at[piece], hold.at[piece], in_sem.at[k]))
+            outs.append(pltpu.make_async_copy(hold.at[piece], target.at[piece], out_sem.at[k]))
+    for copy in ins:
+        copy.start()
+    for arrival, copy in zip(ins, outs):
+        arrival.wait()
+        copy.start()
+    for copy in outs:
+        copy.wait()
+
+
+def hand_over(results):
+    parts = (1, 8, 1)
+    shapes = [jax.ShapeDtypeStruct(x.shape, x.dtype) for x in results]
+    anywhere = [pl.BlockSpec(memory_space=pl.ANY)] * len(shapes)
+    return pl.pallas_call(
+        functools.partial(hand_over_kernel, parts),
+        out_shape=shapes,
+        in_specs=anywhere,
+        out_specs=anywhere,
+        scratch_shapes=[pltpu.VMEM(x.shape, x.dtype) for x in shapes]
+        + [pltpu.SemaphoreType.DMA((sum(parts),))] * 2,
+    )(*results)
 
 
 def local(normed, tile_values, tile_rows, tile_columns, cotangent):
     tokens, features = normed.shape
     width = cotangent.shape[1]
-    pair = jnp.where(tile_columns >= 0, tile_rows * 8 + tile_columns, -1)
-    places = jnp.broadcast_to(pair.reshape(2, 1, 1), (2, 4, TILE)).reshape(1, 8, TILE)
     anywhere = pl.BlockSpec(memory_space=pl.ANY)
     vmem = pl.BlockSpec(memory_space=pltpu.VMEM)
+    smem = pl.BlockSpec(memory_space=pltpu.SMEM)
     f32, bf16 = jnp.float32, jnp.bfloat16
-    sent = jnp.int16 if CODED else f32
-    values, grad_input, update = pl.pallas_call(
+    results = pl.pallas_call(
         kernel,
         out_shape=(
             jax.ShapeDtypeStruct((tokens, width), bf16),
             jax.ShapeDtypeStruct((tokens, features), bf16),
             jax.ShapeDtypeStruct((2, TILE, TILE), bf16),
         ),
-        in_specs=[anywhere] * 4,
+        in_specs=[anywhere, anywhere, anywhere, smem, smem],
         out_specs=(vmem, anywhere, vmem),
         scratch_shapes=[
             pltpu.VMEM((tokens, features), bf16),
@@ -455,17 +487,17 @@
             pltpu.VMEM((RING, features, width), bf16),
             pltpu.VMEM((4, tokens // 4, width), f32),
             pltpu.VMEM((4, tokens // 4, width), f32),
-            pltpu.VMEM((2, 6, tokens // 4, width), sent),
-            pltpu.VMEM((2, 6, tokens // 4, width), sent),
+            pltpu.VMEM((2, 6, tokens // 4, width), jnp.int16),
+            pltpu.VMEM((2, 6, tokens // 4, width), jnp.int16),
             pltpu.VMEM((2, 6, 8, width), f32),
             pltpu.VMEM((2, 6, 8, width), f32),
             pltpu.VMEM((128, TILE, TILE), f32),
             pltpu.VMEM((2, 64, TILE, TILE), f32),
             pltpu.VMEM((64, TILE, TILE), f32),
-            pltpu.VMEM((16, TILE, TILE), f32),
-            pltpu.VMEM((2, 16, TILE, TILE), f32),
-            pltpu.VMEM((4, TILE, TILE), f32),
-            pltpu.VMEM((2, 4, TILE, TILE), f32),
+            *[pltpu.VMEM((6, 8, TILE, TILE), jnp.int16)] * 2,
+            *[pltpu.VMEM((6, 8, 8, TILE), f32)] * 2,
+            *[pltpu.VMEM((6, 2, TILE, TILE), jnp.int16)] * 2,
+            *[pltpu.VMEM((6, 2, 8, TILE), f32)] * 2,
             pltpu.VMEM((2, TILE, TILE), f32),
             pltpu.VMEM((tokens, features), bf16),
             pltpu.SemaphoreType.DMA((7,)),
@@ -476,7 +508,8 @@
         compiler_params=pltpu.CompilerParams(
             collective_id=0, has_side_effects=True, vmem_limit_bytes=67043328
         ),
-    )(normed, cotangent, tile_values.reshape(2, TILE, TILE), places)
+    )(normed, cotangent, tile_values.reshape(2, TILE, TILE), tile_rows, tile_columns)
+    values, grad_input, update = hand_over(results)
     return values, grad_input, update[None]
 
 

time: 108 us -> 97 us (0.90)
  the two profiles are of different devices: /device:TPU:10 before, /device:TPU:1 now
where the time goes in v3:
time: 97 us; the launch traced here: 96.9 us
  Pallas kernels  96.3 us (99%)
    pallas_call x1, Pallas kernels, local(): pl.pallas_call(kernel, out_shape=(jax.ShapeDtypeStruct((tokens, width), b...  92.1 us
    pallas_call x1, Pallas kernels, hand_over(): pl.pallas_call(functools.partial(hand_over_kernel, parts), out_shape=shap...  4.18 us

profile of v3, /device:TPU:1, one launch (start us, length us, event | category | flops | bytes accessed | tf_op | source)
XLA Modules:
  0.0 96.9 jit_solution(1834126920342806195)
XLA Ops:
  0.6 92.1 %shard_map.76 = (bf16[1024,256]{1,0:T(8,128)(2,1)}, bf16[1024,2048]{1,0:T(8,128)(2,1)}, bf16[2,128,128]{2,1,0:T(8,128)(2,1)}) custom-call(bf16[1024,2048]{1,0:T(8,128)(2,1)} %norm_hbm.1, bf16[1024,256]{1,0:T(8,128)(2,1)} %cot_hbm.1, bf16[2,128,128]{2,1,0:T(8,128)(2,1)} %bitcast.2, s32[1,2]{1,0:T(1,128)} %rows_ref.1, s32[1,2]{1,0:T(1,128)} %columns_ref.1), custom_call_target="tpu_custom_call" | custom-call | tf_op jit(solution)/shard_map/pallas_call | solution.py:470
  92.7 4.2 %shard_map.77 = (bf16[1024,256]{1,0:T(8,128)(2,1)}, bf16[1024,2048]{1,0:T(8,128)(2,1)}, bf16[2,128,128]{2,1,0:T(8,128)(2,1)}) custom-call(bf16[1024,256]{1,0:T(8,128)(2,1)} %get-tuple-element.9.refs_0_, bf16[1024,2048]{1,0:T(8,128)(2,1)} %get-tuple-element.10.refs_1_, bf16[2,128,128]{2,1,0:T(8,128)(2,1)} %get-tuple-element.11.refs_2_), custom_call_target="tpu_custom_call" | custom-call | tf_op jit(solution)/shard_map/pallas_call | solution.py:453

commit v4 on v3

--- a/solution.py
+++ b/solution.py
@@ -37,9 +37,9 @@
 
 
 def kernel(
-    norm_hbm, cot_hbm, tiles_hbm, rows_ref, columns_ref, values_ref, gi_hbm, update_ref,
+    norm_hbm, cot_hbm, tiles_hbm, rows_ref, columns_ref, values_ref, gi, update_ref,
     norm, cot, cot_t, tiles, places, table, table_s, weight, own, joint, z_out, z_in, s_out, s_in,
-    grad, packed, core_in, bq_out, bq_in, br_out, br_in, aq_out, aq_in, ar_out, ar_in, zl_in, gi, local_sem, send_sem, recv_sem,
+    grad, packed, core_in, bq_out, bq_in, br_out, br_in, aq_out, aq_in, ar_out, ar_in, pq_out, pq_in, pr_out, pr_in, local_sem, send_sem, recv_sem,
     z_send, z_recv, s_send, s_recv,
 ):
     tokens, features = norm.shape
@@ -126,16 +126,22 @@
         def block(i):
             return origin + i * size
 
-        ups = send_owners(block(index), size, up)
-        downs = send_owners(block(index), size, down)
-        yield
-        arrived(ups)
-        ups = send_owners(block(near(index, -1)), size // 2, up)
-        arrived(downs)
-        downs = send_owners(block(near(index, 1)) + size // 2, size // 2, down)
-        yield
-        arrived(ups)
-        arrived(downs)
+        low_at, high_at = block(index), block(index) + size // 2
+        ups, downs = [], []
+        for to_up, to_down in ((low_at, high_at), (high_at, low_at)):
+            ups.append(send_owners(to_up, size // 2, up))
+            downs.append(send_owners(to_down, size // 2, down))
+        yield
+        arrived(ups[0])
+        ups += [send_owners(block(near(index, -1)), size // 2, up)]
+        arrived(downs[0])
+        downs += [send_owners(block(near(index, 1)) + size // 2, size // 2, down)]
+        yield
+        arrived(ups[1])
+        arrived(downs[1])
+        yield
+        arrived(ups[2])
+        arrived(downs[2])
         yield
 
     def to_core(i):
@@ -167,6 +173,7 @@
     next(first_ring)
     get_norm.wait()
     gradient(t, 0, steps // 4)
+    next(first_ring)
     next(first_ring)
     second_ring = ring_gather(core * RING * 8, 8, b, up_b, down_b)
     next(second_ring)
@@ -179,6 +186,7 @@
     pass_l = send(cot.at[right_t, high], cot.at[right_t, high], left)
     pass_l.start()
     next(second_ring)
+    next(second_ring)
     across += to_core(near(b, -1)) + to_core(near(b, 1))
     next(second_ring)
     across += to_core(near(b, 2))
@@ -198,22 +206,26 @@
         return jnp.maximum(sums[0], where_is), sums[1] + pair_of
 
     zero = jnp.zeros((8, TILE), jnp.int32)
-    where_is, pair_of = lax.fori_loop(0, 64, place, (zero, zero))
+    where_is, pair_of = lax.fori_loop(0, 64, place, (zero, zero), unroll=8)
     table[0:8, :] = where_is
     table[8:16, :] = pair_of
     get_table = pltpu.make_async_copy(table, table_s, local_sem.at[6])
     get_table.start()
     get_table.wait()
 
-    def assemble(r, _):
-        for c in range(8):
-            code = jnp.maximum(table_s[0, r * 8 + c], table_s[4, r * 8 + c])
-            tile = tiles[jnp.maximum(code, 1) - 1]
-            tile = jnp.where(code > 0, tile, jnp.zeros_like(tile))
-            weight[c // 2, rows(r * TILE, TILE, TILE), (c % 2) * TILE : (c % 2 + 1) * TILE] = tile
-        return 0
-
-    lax.fori_loop(0, features // TILE, assemble, 0)
+    def assemble(q):
+        def one(r, _):
+            for j in range(2):
+                pair = r * 8 + q * 2 + j
+                code = jnp.maximum(table_s[0, pair], table_s[4, pair])
+                tile = tiles[jnp.maximum(code, 1) - 1]
+                tile = jnp.where(code > 0, tile, jnp.zeros_like(tile))
+                weight[q, rows(r * TILE, TILE, TILE), j * TILE : (j + 1) * TILE] = tile
+            return 0
+
+        lax.fori_loop(0, features // TILE, one, 0, unroll=2)
+
+    assemble(far_t)
 
     chunk = tokens // 4
 
@@ -245,12 +257,15 @@
     def received(way, j):
         return decode(z_in[way, j], s_in[way, j])
 
-    def to_far(i, _):
-        way, j = div(i, 2), rem(i, 2)
-        post(way, j, partial(2, i))
-        return 0
-
-    lax.fori_loop(0, 4, to_far, 0)
+    def to_far(j):
+        def one(way, _):
+            post(way, j, partial(2, way * 2 + j))
+            return 0
+
+        lax.fori_loop(0, 2, one, 0)
+
+    to_far(0)
+    to_far(1)
 
     arrived([pass_r, pass_l])
     turn(far_t)
@@ -264,7 +279,7 @@
             packed[side, slot] = jnp.where(pair >= 0, tile, jnp.zeros_like(tile))
             return 0
 
-        lax.fori_loop(0, 16, one, 0)
+        lax.fori_loop(0, 16, one, 0, unroll=4)
 
     core_copies = []
     for by in (2, 1, -1, 0):
@@ -274,8 +289,8 @@
         copy = send(packed.at[1, piece], core_in.at[piece], other_core)
         copy.start()
         core_copies.append(copy)
-    for i in range(RING):
-        pack(0, core, i)
+    for by in (2, 1, -1, 0):
+        pack(0, core, near(b, by))
 
     def input_block(n, _):
         th, block = div(n, 8), rem(n, 8)
@@ -289,10 +304,6 @@
 
     def grad_input(th):
         lax.fori_loop(th * 8, th * 8 + 8, input_block, 0)
-        at_rows = pl.ds(th * half, half)
-        put = pltpu.make_async_copy(gi.at[at_rows], gi_hbm.at[at_rows], local_sem.at[3 + th])
-        put.start()
-        return put
 
     def add_into(dst, dst_at, src, src_at, size):
         def one(s, _):
@@ -363,6 +374,9 @@
     over_b = ring_scatter(16, 0, b, up_b, down_b, bq_out, bq_in, br_out, br_in, add_core)
     next(over_b)
 
+    for q in (left_t, right_t, t):
+        assemble(q)
+
     def to_near(i, _):
         way, j = div(i, 2), rem(i, 2)
         post(way, 2 + j, partial(1 + 2 * way, (1 - way) * 2 + j))
@@ -388,15 +402,22 @@
         return 0
 
     lax.fori_loop(0, 4, pass_on, 0)
-    puts = [grad_input(0)]
+    grad_input(0)
     next(over_b)
-    puts += [grad_input(1)]
+    grad_input(1)
     next(over_b)
     for _ in ring_scatter(4, b * 16, a, up_a, down_a, aq_out, aq_in, ar_out, ar_in, lambda by: None):
         pass
     kept = b * 16 + a * 4
-    zl_copy = send(acc.at[pl.ds(kept + 2 * (1 - zl), 2)], zl_in, other_zl)
-    zl_copy.start()
+
+    def for_pair(k, _):
+        pq_out[k], pr_out[k] = encode(acc[kept + 2 * (1 - zl) + k])
+        return 0
+
+    lax.fori_loop(0, 2, for_pair, 0)
+    zl_copies = send(pq_out, pq_in, other_zl), send(pr_out, pr_in, other_zl)
+    for copy in zl_copies:
+        copy.start()
 
     def finish(i, _):
         h, j = div(i, 2), rem(i, 2)
@@ -408,13 +429,11 @@
         return 0
 
     lax.fori_loop(0, 4, finish, 0)
-    zl_copy.wait_recv()
+    arrived(zl_copies)
     for k in range(2):
-        tile = acc[kept + 2 * zl + k] + zl_in[k]
+        tile = acc[kept + 2 * zl + k] + decode(pq_in[k], pr_in[k])
         mean = jnp.sum(tile * tile, axis=(0, 1), keepdims=True) / (TILE * TILE)
         update_ref[k] = (tile * lax.rsqrt(mean + 1e-06)).T.astype(jnp.bfloat16)
-    for put in puts:
-        put.wait()
     for copy in started:
         copy.wait_send()
     for way in range(2):
@@ -423,40 +442,33 @@
                 copy.wait_send()
 
 
-COPIES = 61
+COPIES = 70
 
 
 def hand_over_kernel(parts, *refs):
     count = len(parts)
-    sources, targets, held = refs[:count], refs[count : 2 * count], refs[2 * count : 3 * count]
-    in_sem, out_sem = refs[3 * count :]
-    ins, outs = [], []
-    for source, target, hold, number in zip(sources, targets, held, parts):
+    sources, targets, sem = refs[:count], refs[count : 2 * count], refs[2 * count]
+    copies = []
+    for source, target, number in zip(sources, targets, parts):
         size = source.shape[0] // number
         for i in range(number):
-            piece, k = pl.ds(i * size, size), len(ins)
-            ins.append(pltpu.make_async_copy(source.at[piece], hold.at[piece], in_sem.at[k]))
-            outs.append(pltpu.make_async_copy(hold.at[piece], target.at[piece], out_sem.at[k]))
-    for copy in ins:
+            piece = pl.ds(i * size, size)
+            copies.append(pltpu.make_async_copy(source.at[piece], target.at[piece], sem.at[len(copies)]))
+    for copy in copies:
         copy.start()
-    for arrival, copy in zip(ins, outs):
-        arrival.wait()
-        copy.start()
-    for copy in outs:
+    for copy in copies:
         copy.wait()
 
 
 def hand_over(results):
-    parts = (1, 8, 1)
-    shapes = [jax.ShapeDtypeStruct(x.shape, x.dtype) for x in results]
-    anywhere = [pl.BlockSpec(memory_space=pl.ANY)] * len(shapes)
+    parts = (1, 4, 1)
     return pl.pallas_call(
         functools.partial(hand_over_kernel, parts),
-        out_shape=shapes,
-        in_specs=anywhere,
-        out_specs=anywhere,
-        scratch_shapes=[pltpu.VMEM(x.shape, x.dtype) for x in shapes]
-        + [pltpu.SemaphoreType.DMA((sum(parts),))] * 2,
+        out_shape=[jax.ShapeDtypeStruct(x.shape, x.dtype) for x in results],
+        in_specs=[pl.BlockSpec(memory_space=pltpu.VMEM)] * len(results),
+        out_specs=[pl.BlockSpec(memory_space=pl.ANY)] * len(results),
+        scratch_shapes=[pltpu.SemaphoreType.DMA((sum(parts),))],
+        compiler_params=pltpu.CompilerParams(vmem_limit_bytes=1 << 20),
     )(*results)
 
 
@@ -470,12 +482,12 @@
     results = pl.pallas_call(
         kernel,
         out_shape=(
-            jax.ShapeDtypeStruct((tokens, width), bf16),
-            jax.ShapeDtypeStruct((tokens, features), bf16),
-            jax.ShapeDtypeStruct((2, TILE, TILE), bf16),
+            pltpu.VMEM((tokens, width), bf16),
+            pltpu.VMEM((tokens, features), bf16),
+            pltpu.VMEM((2, TILE, TILE), bf16),
         ),
         in_specs=[anywhere, anywhere, anywhere, smem, smem],
-        out_specs=(vmem, anywhere, vmem),
+        out_specs=(vmem, vmem, vmem),
         scratch_shapes=[
             pltpu.VMEM((tokens, features), bf16),
             pltpu.VMEM((RING, tokens, width), bf16),
@@ -498,15 +510,15 @@
             *[pltpu.VMEM((6, 8, 8, TILE), f32)] * 2,
             *[pltpu.VMEM((6, 2, TILE, TILE), jnp.int16)] * 2,
             *[pltpu.VMEM((6, 2, 8, TILE), f32)] * 2,
-            pltpu.VMEM((2, TILE, TILE), f32),
-            pltpu.VMEM((tokens, features), bf16),
+            *[pltpu.VMEM((2, TILE, TILE), jnp.int16)] * 2,
+            *[pltpu.VMEM((2, 8, TILE), f32)] * 2,
             pltpu.SemaphoreType.DMA((7,)),
             pltpu.SemaphoreType.DMA((COPIES,)),
             pltpu.SemaphoreType.DMA((COPIES,)),
             *[pltpu.SemaphoreType.DMA((2, 6))] * 4,
         ],
         compiler_params=pltpu.CompilerParams(
-            collective_id=0, has_side_effects=True, vmem_limit_bytes=67043328
+            collective_id=0, has_side_effects=True, vmem_limit_bytes=50 << 20
         ),
     )(normed, cotangent, tile_values.reshape(2, TILE, TILE), tile_rows, tile_columns)
     values, grad_input, update = hand_over(results)

time: 97 us -> 92 us (0.948)
  Pallas kernels: 96.3 us -> 91.3 us
    pallas_call x2, Pallas kernels: 96.3 us -> 91.3 us  [the longest x1 89.1 us: local(): pl.pallas_call(kernel, out_shape=(pltpu.VMEM((tokens, width), bf16), pltp...]
where the time goes in v4:
time: 92 us
  Pallas kernels  91.3 us (99%)
    pallas_call x1, Pallas kernels, local(): pl.pallas_call(kernel, out_shape=(pltpu.VMEM((tokens, width), bf16), pltp...  89.1 us
    pallas_call x1, Pallas kernels, hand_over(): pl.pallas_call(functools.partial(hand_over_kernel, parts), out_shape=[jax...  2.24 us

profile of v4, /device:TPU:1, one launch (start us, length us, event | category | flops | bytes accessed | tf_op | source)
XLA Modules:
  0.0 92.0 jit_solution(5418499344180940725)
XLA Ops:
  0.6 89.1 %shard_map.76 = (bf16[1024,256]{1,0:T(8,128)(2,1)S(1)}, bf16[1024,2048]{1,0:T(8,128)(2,1)S(1)}, bf16[2,128,128]{2,1,0:T(8,128)(2,1)S(1)}) custom-call(bf16[1024,2048]{1,0:T(8,128)(2,1)} %norm_hbm.1, bf16[1024,256]{1,0:T(8,128)(2,1)} %cot_hbm.1, bf16[2,128,128]{2,1,0:T(8,128)(2,1)} %bitcast.2, s32[1,2]{1,0:T(1,128)} %rows_ref.1, s32[1,2]{1,0:T(1,128)} %columns_ref.1), custom_call_target="tpu_custom_call" | custom-call | tf_op jit(solution)/shard_map/pallas_call | solution.py:482
  89.7 2.2 %shard_map.77 = (bf16[1024,256]{1,0:T(8,128)(2,1)}, bf16[1024,2048]{1,0:T(8,128)(2,1)}, bf16[2,128,128]{2,1,0:T(8,128)(2,1)}) custom-call(bf16[1024,256]{1,0:T(8,128)(2,1)S(1)} %get-tuple-element.9.refs_0_, bf16[1024,2048]{1,0:T(8,128)(2,1)S(1)} %get-tuple-element.10.refs_1_, bf16[2,128,128]{2,1,0:T(8,128)(2,1)S(1)} %get-tuple-element.11.refs_2_), custom_call_target="tpu_custom_call" | custom-call | tf_op jit(solution)/shard_map/pallas_call | solution.py:465

commit v5 on v4

--- a/solution.py
+++ b/solution.py
@@ -24,15 +24,17 @@
     return pl.ds(pl.multiple_of(start, unit), size)
 
 
-def encode(x):
-    groups = x.reshape(8, x.shape[0] // 8, x.shape[1])
+def encode(x, count=8):
+    groups = x.reshape(count, x.shape[0] // count, x.shape[1])
     largest = jnp.maximum(jnp.max(jnp.abs(groups), axis=1), 1e-30)
     whole = lax.round(groups * (32767.0 / largest)[:, None, :], lax.RoundingMethod.TO_NEAREST_EVEN)
     return whole.astype(jnp.int32).astype(jnp.int16).reshape(x.shape), largest * (1 / 32767.0)
 
 
 def decode(coded, scales):
-    groups = coded.astype(jnp.int32).astype(jnp.float32).reshape(8, coded.shape[0] // 8, coded.shape[1])
+    groups = coded.astype(jnp.int32).astype(jnp.float32).reshape(
+        scales.shape[0], coded.shape[0] // scales.shape[0], coded.shape[1]
+    )
     return (groups * scales[:, None, :]).reshape(coded.shape)
 
 
@@ -193,9 +195,6 @@
     cot_r[1].wait_recv()
     turn(left_t)
     gradient(left_t, 0, steps)
-    cot_l[1].wait_recv()
-    turn(right_t)
-    gradient(right_t, 0, steps)
     arrived(across)
 
 
@@ -250,7 +249,7 @@
         return copies
 
     def post(way, j, x):
-        z_out[way, j], s_out[way, j] = encode(x)
+        z_out[way, j], s_out[way, j] = encode(x, 4)
         for copy in message(way, j):
             copy.start()
 
@@ -266,6 +265,9 @@
 
     to_far(0)
     to_far(1)
+    cot_l[1].wait_recv()
+    turn(right_t)
+    gradient(right_t, 0, steps)
 
     arrived([pass_r, pass_l])
     turn(far_t)
@@ -302,8 +304,8 @@
         gi[at_rows, at_cols] = out.astype(jnp.bfloat16)
         return 0
 
-    def grad_input(th):
-        lax.fori_loop(th * 8, th * 8 + 8, input_block, 0)
+    def grad_input(start, stop):
+        lax.fori_loop(start, stop, input_block, 0)
 
     def add_into(dst, dst_at, src, src_at, size):
         def one(s, _):
@@ -372,18 +374,20 @@
         add_into(acc, start, core_in, start, 16)
 
     over_b = ring_scatter(16, 0, b, up_b, down_b, bq_out, bq_in, br_out, br_in, add_core)
-    next(over_b)
-
     for q in (left_t, right_t, t):
         assemble(q)
 
-    def to_near(i, _):
-        way, j = div(i, 2), rem(i, 2)
-        post(way, 2 + j, partial(1 + 2 * way, (1 - way) * 2 + j))
-        return 0
-
-    lax.fori_loop(0, 4, to_near, 0)
-
+    def to_near(j):
+        def one(way, _):
+            post(way, 2 + j, partial(1 + 2 * way, (1 - way) * 2 + j))
+            return 0
+
+        lax.fori_loop(0, 2, one, 0)
+
+    to_near(0)
+    next(over_b)
+    next(over_b)
+    to_near(1)
     next(over_b)
 
     def rest(i, _):
@@ -392,7 +396,6 @@
         return 0
 
     lax.fori_loop(0, 4, rest, 0)
-
 
     def pass_on(i, _):
         way, j = div(i, 2), rem(i, 2)
@@ -402,12 +405,14 @@
         return 0
 
     lax.fori_loop(0, 4, pass_on, 0)
-    grad_input(0)
     next(over_b)
-    grad_input(1)
-    next(over_b)
-    for _ in ring_scatter(4, b * 16, a, up_a, down_a, aq_out, aq_in, ar_out, ar_in, lambda by: None):
-        pass
+    over_a = ring_scatter(4, b * 16, a, up_a, down_a, aq_out, aq_in, ar_out, ar_in, lambda by: None)
+    next(over_a)
+    next(over_a)
+    grad_input(0, 3)
+    next(over_a)
+    grad_input(3, 6)
+    next(over_a)
     kept = b * 16 + a * 4
 
     def for_pair(k, _):
@@ -418,6 +423,8 @@
     zl_copies = send(pq_out, pq_in, other_zl), send(pr_out, pr_in, other_zl)
     for copy in zl_copies:
         copy.start()
+
+    grad_input(6, 16)
 
     def finish(i, _):
         h, j = div(i, 2), rem(i, 2)
@@ -501,8 +508,8 @@
             pltpu.VMEM((4, tokens // 4, width), f32),
             pltpu.VMEM((2, 6, tokens // 4, width), jnp.int16),
             pltpu.VMEM((2, 6, tokens // 4, width), jnp.int16),
-            pltpu.VMEM((2, 6, 8, width), f32),
-            pltpu.VMEM((2, 6, 8, width), f32),
+            pltpu.VMEM((2, 6, 4, width), f32),
+            pltpu.VMEM((2, 6, 4, width), f32),
             pltpu.VMEM((128, TILE, TILE), f32),
             pltpu.VMEM((2, 64, TILE, TILE), f32),
             pltpu.VMEM((64, TILE, TILE), f32),

time: 92 us -> 90.1 us (0.979)
  Pallas kernels: 91.3 us -> 89.4 us
    pallas_call x1, Pallas kernels: 89.1 us -> 87.1 us  [local(): pl.pallas_call(kernel, out_shape=(pltpu.VMEM((tokens, width), bf16), pltp...]
where the time goes in v5:
time: 90.1 us; the launch traced here: 90 us
  Pallas kernels  89.4 us (99%)
    pallas_call x1, Pallas kernels, local(): pl.pallas_call(kernel, out_shape=(pltpu.VMEM((tokens, width), bf16), pltp...  87.1 us
    pallas_call x1, Pallas kernels, hand_over(): pl.pallas_call(functools.partial(hand_over_kernel, parts), out_shape=[jax...  2.24 us

profile of v5, /device:TPU:1, one launch (start us, length us, event | category | flops | bytes accessed | tf_op | source)
XLA Modules:
  0.0 90.0 jit_solution(3866846735957213457)
XLA Ops:
  0.6 87.1 %shard_map.76 = (bf16[1024,256]{1,0:T(8,128)(2,1)S(1)}, bf16[1024,2048]{1,0:T(8,128)(2,1)S(1)}, bf16[2,128,128]{2,1,0:T(8,128)(2,1)S(1)}) custom-call(bf16[1024,2048]{1,0:T(8,128)(2,1)} %norm_hbm.1, bf16[1024,256]{1,0:T(8,128)(2,1)} %cot_hbm.1, bf16[2,128,128]{2,1,0:T(8,128)(2,1)} %bitcast.2, s32[1,2]{1,0:T(1,128)} %rows_ref.1, s32[1,2]{1,0:T(1,128)} %columns_ref.1), custom_call_target="tpu_custom_call" | custom-call | tf_op jit(solution)/shard_map/pallas_call | solution.py:489
  87.8 2.2 %shard_map.77 = (bf16[1024,256]{1,0:T(8,128)(2,1)}, bf16[1024,2048]{1,0:T(8,128)(2,1)}, bf16[2,128,128]{2,1,0:T(8,128)(2,1)}) custom-call(bf16[1024,256]{1,0:T(8,128)(2,1)S(1)} %get-tuple-element.9.refs_0_, bf16[1024,2048]{1,0:T(8,128)(2,1)S(1)} %get-tuple-element.10.refs_1_, bf16[2,128,128]{2,1,0:T(8,128)(2,1)S(1)} %get-tuple-element.11.refs_2_), custom_call_target="tpu_custom_call" | custom-call | tf_op jit(solution)/shard_map/pallas_call | solution.py:472
